TPU v7x, 32 devices: a whole 2x2x4 slice. The times are simulated.
32 devices in a mesh: groups: 2 (over x), ctx: 16 (over z, y, core).
Axes of the slice: x: 2, y: 2, z: 4, core: 2. Of those that a mesh axis runs over, the one named last changes fastest.
Arguments:
- queries: bfloat16 [4096, 4096], P(('groups', 'ctx')), parts along dimension 0, may hold values from -130 to 130
- keys_values: bfloat16 [4096, 1024], P(('groups', 'ctx')), parts along dimension 0, may hold values from -25 to 25
- out_grad: bfloat16 [4096, 4096], P(('groups', 'ctx')), parts along dimension 0, may hold values from -6 to 6
- key_blocks: int32 [32, 3], P('groups'), parts along dimension 0, may hold values from 0 to 15, as said below
- key_count: int32 [32], P('groups'), parts along dimension 0, may hold values from 1 to 3, as said below
- block_at_slot: int32 [32], P('groups'), parts along dimension 0, may hold values from 0 to 15, as said below
Outputs:
- attended: bfloat16 [4096, 4096], P(('groups', 'ctx')), parts along dimension 0
- query_grad: bfloat16 [4096, 4096], P(('groups', 'ctx')), parts along dimension 0
- kv_grad: bfloat16 [4096, 1024], P(('groups', 'ctx')), parts along dimension 0
There are 2 independent parts, one for each index of `groups`. A program takes and returns all parts, laid end to end along the dimension named above; each array names one. Nothing has to cross between parts.
Inputs may be any that keep to these rules, and one draw needn't show every extreme that they name: `block_at_slot`: A permutation of the block ids. `key_blocks`: each row lists 3 distinct block ids, the first being the row's own block. Every listed block sits at most 2 slots away from the row's block in the layout of block_at_slot, and some live entry sits exactly 2 slots away. `key_count`: some row has 3 live entries.
All inputs are finite; a program needn't handle non-finite values.
Results may differ from a plain program's by a relative error of at most 0.02.
Values may be sent and summed in bfloat16 or wider, within the bound.
A program may use at most 128 MiB of HBM per device.

v0:
```python
import functools

import jax
import jax.numpy as jnp
from jax import lax
from jax.experimental import pallas as pl
from jax.experimental.pallas import tpu as pltpu
from jax.sharding import PartitionSpec as P

HEAD = 128
OFFSETS = (-2, -1, 1, 2)
LOG2E = 1.4426950408889634
NEG = -1e30
NT = (((1,), (1,)), ((), ()))


def kernel(
    n, groups, repeats,
    blocks_ref, count_ref, slot_ref, q_hbm, kv_hbm, do_hbm,
    att_hbm, dq_hbm, kvg_hbm,
    q, kv, do, att, dq, kvg, near, own_grad, gsend, grecv,
    in_sem, kv_sem, out_sem, kvg_sem, near_send, near_recv, grad_send, grad_recv,
):
    rows = q.shape[0]
    wide = repeats * HEAD
    kv_width = groups * HEAD
    scale = HEAD ** (-0.5)
    me = lax.axis_index("ctx")

    def exists(o):
        return jnp.logical_and(me + OFFSETS[o] >= 0, me + OFFSETS[o] < n)

    def target(o):
        return {"ctx": me + OFFSETS[o]}

    def column(g, width):
        return pl.ds(pl.multiple_of(g * width, width), width)

    def near_copy(g, o, part):
        return pltpu.make_async_remote_copy(
            src_ref=kv_hbm.at[:, pl.ds(pl.multiple_of(part * kv_width + g * HEAD, HEAD), HEAD)],
            dst_ref=near.at[g, 3 - o, part],
            send_sem=near_send.at[g, o, part],
            recv_sem=near_recv.at[g, 3 - o, part],
            device_id=target(o),
            device_id_type=pl.DeviceIdType.MESH,
        )

    def grad_copy(g, o):
        return pltpu.make_async_remote_copy(
            src_ref=gsend.at[g, o],
            dst_ref=grecv.at[g, 3 - o],
            send_sem=grad_send.at[g, o],
            recv_sem=grad_recv.at[g, 3 - o],
            device_id=target(o),
            device_id_type=pl.DeviceIdType.MESH,
        )

    def load_copies(g):
        return (
            pltpu.make_async_copy(q_hbm.at[:, column(g, wide)], q.at[:, column(g, wide)], in_sem.at[g, 0]),
            pltpu.make_async_copy(do_hbm.at[:, column(g, wide)], do.at[:, column(g, wide)], in_sem.at[g, 1]),
        )

    def store_copies(g):
        return (
            pltpu.make_async_copy(att.at[:, column(g, wide)], att_hbm.at[:, column(g, wide)], out_sem.at[g, 0]),
            pltpu.make_async_copy(dq.at[:, column(g, wide)], dq_hbm.at[:, column(g, wide)], out_sem.at[g, 1]),
        )

    kv_load = pltpu.make_async_copy(kv_hbm, kv, kv_sem)

    barrier = pltpu.get_barrier_semaphore()
    arrivals = jnp.int32(0)
    for o in range(4):
        there = exists(o)
        arrivals = arrivals + there.astype(jnp.int32)

        @pl.when(there)
        def _():
            pl.semaphore_signal(barrier, inc=1, device_id=target(o), device_id_type=pl.DeviceIdType.MESH)

        @pl.when(jnp.logical_not(there))
        def _():
            near[:, o] = jnp.zeros((groups, 2, rows, HEAD), near.dtype)
            grecv[:, o] = jnp.zeros((groups, 2, rows, HEAD), grecv.dtype)

    kv_load.start()
    for g in range(groups):
        for copy in load_copies(g):
            copy.start()
    pl.semaphore_wait(barrier, arrivals)

    for g in range(groups):
        for o in (3, 0, 2, 1):

            @pl.when(exists(o))
            def _():
                near_copy(g, o, 0).start()
                near_copy(g, o, 1).start()

    own_block = slot_ref[me]
    live_count = count_ref[own_block]
    chosen = []
    bias = []
    for j in (1, 2):
        wanted = blocks_ref[own_block, j]
        hits = []
        for o in range(4):
            there = jnp.clip(me + OFFSETS[o], 0, n - 1)
            hits.append(exists(o) & (slot_ref[there] == wanted) & (live_count > j))
        chosen.append(hits)
        bias.append(jnp.where(hits[0] | hits[1] | hits[2] | hits[3], 0.0, NEG).astype(jnp.float32))

    kv_load.wait()

    def pick(g, part, hits):
        value = near[g, 0, part]
        for o in range(1, 4):
            value = jnp.where(hits[o], near[g, o, part], value)
        return value

    def step(g, carry):
        for copy in load_copies(g):
            copy.wait()
        for o in range(4):

            @pl.when(exists(3 - o))
            def _():
                near_copy(g, o, 0).wait_recv()
                near_copy(g, o, 1).wait_recv()

        own_key = kv[:, pl.ds(pl.multiple_of(g * HEAD, HEAD), HEAD)]
        own_value = kv[:, pl.ds(pl.multiple_of(kv_width + g * HEAD, HEAD), HEAD)]
        keys = jnp.concatenate([own_key, pick(g, 0, chosen[0]), pick(g, 0, chosen[1])], axis=0)
        values = jnp.concatenate([own_value, pick(g, 1, chosen[0]), pick(g, 1, chosen[1])], axis=0)
        keys_t = keys.T
        values_t = values.T
        key_grad = jnp.zeros((3 * rows, HEAD), jnp.float32)
        value_grad = jnp.zeros((3 * rows, HEAD), jnp.float32)
        for pair in range(repeats // 2):
            starts = [pl.multiple_of(g * wide + (2 * pair + i) * HEAD, HEAD) for i in range(2)]
            q2 = jnp.concatenate([q[:, pl.ds(s, HEAD)] for s in starts], axis=0)
            do2 = jnp.concatenate([do[:, pl.ds(s, HEAD)] for s in starts], axis=0)
            raw = lax.dot_general(keys, q2, NT, preferred_element_type=jnp.float32) * (scale * LOG2E)
            scores = jnp.concatenate(
                [raw[:rows], raw[rows : 2 * rows] + bias[0], raw[2 * rows :] + bias[1]], axis=0
            )
            best = jnp.max(scores, axis=0, keepdims=True)
            weights = jnp.exp2(scores - best)
            total = jnp.sum(weights, axis=0, keepdims=True)
            probs = weights * (1.0 / total)
            rounded = probs.astype(jnp.bfloat16)
            prob_grads = lax.dot_general(values, do2, NT, preferred_element_type=jnp.float32)
            delta = jnp.sum(probs * prob_grads, axis=0, keepdims=True)
            score_grads = (probs * (prob_grads - delta)).astype(jnp.bfloat16)
            mixed = jnp.dot(values_t, rounded, preferred_element_type=jnp.float32)
            query_grad = jnp.dot(keys_t, score_grads, preferred_element_type=jnp.float32) * scale
            mixed = mixed.astype(jnp.bfloat16).T
            query_grad = query_grad.astype(jnp.bfloat16).T
            for i in range(2):
                att[:, pl.ds(starts[i], HEAD)] = mixed[i * rows : (i + 1) * rows]
                dq[:, pl.ds(starts[i], HEAD)] = query_grad[i * rows : (i + 1) * rows]
            key_grad = key_grad + jnp.dot(score_grads, q2, preferred_element_type=jnp.float32)
            value_grad = value_grad + jnp.dot(rounded, do2, preferred_element_type=jnp.float32)
        for part, grad in ((0, key_grad * scale), (1, value_grad)):
            own_grad[g, part] = grad[:rows]
            for o in range(4):
                gsend[g, o, part] = jnp.where(
                    chosen[0][o], grad[rows : 2 * rows], jnp.where(chosen[1][o], grad[2 * rows :], 0.0)
                ).astype(jnp.bfloat16)
        for o in (3, 0, 2, 1):

            @pl.when(exists(o))
            def _():
                grad_copy(g, o).start()

        for copy in store_copies(g):
            copy.start()
        return carry

    lax.fori_loop(0, groups, step, 0)

    def finish(g, carry):
        for o in range(4):

            @pl.when(exists(3 - o))
            def _():
                grad_copy(g, o).wait_recv()

        for part in range(2):
            total = own_grad[g, part]
            for o in range(4):
                total = total + grecv[g, o, part].astype(jnp.float32)
            kvg[:, pl.ds(pl.multiple_of(part * kv_width + g * HEAD, HEAD), HEAD)] = total.astype(jnp.bfloat16)
        return carry

    lax.fori_loop(0, groups, finish, 0)
    kvg_store = pltpu.make_async_copy(kvg, kvg_hbm, kvg_sem)
    kvg_store.start()

    def drain(g, carry):
        for o in range(4):

            @pl.when(exists(o))
            def _():
                near_copy(g, o, 0).wait_send()
                near_copy(g, o, 1).wait_send()
                grad_copy(g, o).wait_send()

        for copy in store_copies(g):
            copy.wait()
        return carry

    lax.fori_loop(0, groups, drain, 0)
    kvg_store.wait()


def body(queries, keys_values, out_grad, key_blocks, key_count, block_at_slot):
    n = lax.axis_size("ctx")
    rows, width = queries.shape
    kv_width = keys_values.shape[1] // 2
    groups = kv_width // HEAD
    repeats = width // kv_width
    anywhere = pl.BlockSpec(memory_space=pl.ANY)
    scalars = pl.BlockSpec(memory_space=pltpu.SMEM)
    wide = pltpu.VMEM((rows, width), jnp.bfloat16)
    narrow = pltpu.VMEM((rows, 2 * kv_width), jnp.bfloat16)
    ring = pltpu.VMEM((groups, 4, 2, rows, HEAD), jnp.bfloat16)
    dma = pltpu.SemaphoreType.DMA
    return pl.pallas_call(
        functools.partial(kernel, n, groups, repeats),
        out_shape=(
            jax.ShapeDtypeStruct((rows, width), jnp.bfloat16),
            jax.ShapeDtypeStruct((rows, width), jnp.bfloat16),
            jax.ShapeDtypeStruct((rows, 2 * kv_width), jnp.bfloat16),
        ),
        in_specs=[scalars] * 3 + [anywhere] * 3,
        out_specs=(anywhere, anywhere, anywhere),
        scratch_shapes=[
            wide, narrow, wide, wide, wide, narrow,
            ring, pltpu.VMEM((groups, 2, rows, HEAD), jnp.float32), ring, ring,
            dma((groups, 2)), dma, dma((groups, 2)), dma,
            dma((groups, 4, 2)), dma((groups, 4, 2)), dma((groups, 4)), dma((groups, 4)),
        ],
        compiler_params=pltpu.CompilerParams(
            collective_id=0, has_side_effects=True, vmem_limit_bytes=40 * 1024 * 1024
        ),
    )(key_blocks, key_count, block_at_slot, queries, keys_values, out_grad)


def solution(mesh):
    sharded = P(("groups", "ctx"), None)
    return jax.shard_map(
        body,
        mesh=mesh,
        in_specs=(sharded, sharded, sharded, P("groups", None), P("groups"), P("groups")),
        out_specs=(sharded, sharded, sharded),
        check_vma=False,
    )
```

profile of v0, /device:TPU:20, one launch (start us, length us, event | category | flops | bytes accessed | tf_op | source)
XLA Modules:
  0.0 50.0 jit_solution(9938465047194928562)
XLA Ops:
  0.6 0.0 copy-start.4
  0.6 0.0 copy-start.3
  0.7 0.8 %copy.9.blocks_ref = s32[16,3]{1,0:T(8,128)S(1)} copy(s32[16,3]{0,1:T(4,128)} %param.9) | data formatting | bytes 384 | tf_op args[3]
  1.4 0.0 copy-done.4
  1.4 0.0 copy-done.3
  1.4 0.0 copy-start
  1.4 1.2 %copy-done = bf16[128,4096]{1,0:T(8,128)(2,1)S(1)} copy-done((bf16[128,4096]{1,0:T(8,128)(2,1)S(1)}, bf16[128,4096]{1,0:T(8,128)(2,1)}, u32[]{:S(2)}) %copy-start) | copy-done | bytes 1048600
  2.7 0.0 copy-start.1
  2.7 1.2 %copy-done.1 = bf16[128,4096]{1,0:T(8,128)(2,1)S(1)} copy-done((bf16[128,4096]{1,0:T(8,128)(2,1)S(1)}, bf16[128,4096]{1,0:T(8,128)(2,1)}, u32[]{:S(2)}) %copy-start.1) | copy-done | bytes 1048600
  3.9 0.0 copy-start.2
  3.9 0.9 %copy-done.2 = bf16[128,1024]{1,0:T(8,128)(2,1)S(1)} copy-done((bf16[128,1024]{1,0:T(8,128)(2,1)S(1)}, bf16[128,1024]{1,0:T(8,128)(2,1)}, u32[]{:S(2)}) %copy-start.2) | copy-done | bytes 262168
  4.8 42.6 %shard_map.85 = (bf16[128,4096]{1,0:T(8,128)(2,1)S(1)}, bf16[128,4096]{1,0:T(8,128)(2,1)S(1)}, bf16[128,1024]{1,0:T(8,128)(2,1)S(1)}) custom-call(s32[16,3]{1,0:T(8,128)S(1)} %copy.9.blocks_ref, s32[16]{0:T(128)S(1)} %copy-done.3, s32[16]{0:T(128)S(1)} %copy-done.4, bf16[128,4096]{1,0:T(8,128)(2,1)S(1)} %copy-done, bf16[128,1024]{1,0:T(8,128)(2,1)S(1)} %copy-done.2, ...), custom_call_target="tpu_custom_call" | custom-call | tf_op jit(solution)/shard_map/pallas_call | solution.py:231
  47.4 1.0 %copy.13 = bf16[128,4096]{1,0:T(8,128)(2,1)} copy(bf16[128,4096]{1,0:T(8,128)(2,1)S(1)} %get-tuple-element.6) | data formatting | bytes 2097152
  48.4 1.0 %copy.14 = bf16[128,4096]{1,0:T(8,128)(2,1)} copy(bf16[128,4096]{1,0:T(8,128)(2,1)S(1)} %get-tuple-element.7) | data formatting | bytes 2097152
  49.3 0.7 %copy.15 = bf16[128,1024]{1,0:T(8,128)(2,1)} copy(bf16[128,1024]{1,0:T(8,128)(2,1)S(1)} %get-tuple-element.8) | data formatting | bytes 524288
Async XLA Ops:
  0.6 0.8 %copy-start.4 = (s32[16]{0:T(128)S(1)}, s32[16]{0:T(128)}, u32[]{:S(2)}) copy-start(s32[16]{0:T(128)} %slot_ref.1) | copy-start | bytes 196
  0.6 0.8 %copy-start.3 = (s32[16]{0:T(128)S(1)}, s32[16]{0:T(128)}, u32[]{:S(2)}) copy-start(s32[16]{0:T(128)} %count_ref.1) | copy-start | bytes 196
  1.4 1.2 %copy-start = (bf16[128,4096]{1,0:T(8,128)(2,1)S(1)}, bf16[128,4096]{1,0:T(8,128)(2,1)}, u32[]{:S(2)}) copy-start(bf16[128,4096]{1,0:T(8,128)(2,1)} %q_hbm.1) | copy-start | bytes 3145732
  2.7 1.2 %copy-start.1 = (bf16[128,4096]{1,0:T(8,128)(2,1)S(1)}, bf16[128,4096]{1,0:T(8,128)(2,1)}, u32[]{:S(2)}) copy-start(bf16[128,4096]{1,0:T(8,128)(2,1)} %do_hbm.1) | copy-start | bytes 3145732
  3.9 0.9 %copy-start.2 = (bf16[128,1024]{1,0:T(8,128)(2,1)S(1)}, bf16[128,1024]{1,0:T(8,128)(2,1)}, u32[]{:S(2)}) copy-start(bf16[128,1024]{1,0:T(8,128)(2,1)} %kv_hbm.1) | copy-start | bytes 786436
where the time goes:
time: 50.3 us; the launch traced here: 50 us
  Pallas kernels  42.6 us (85%)
  local copies, waits for them, and re-layouts  6.82 us (14%)
  between operations  0.66 us (1%)
    pallas_call x1, Pallas kernels, body(): pl.pallas_call(functools.partial(kernel, n, groups, repeats), out_shape=(...  42.6 us
    unnamed x14, local copies, waits for them, and re-layouts  6.82 us

commit v1 on v0

--- a/solution.py
+++ b/solution.py
@@ -30,31 +30,86 @@
     def exists(o):
         return jnp.logical_and(me + OFFSETS[o] >= 0, me + OFFSETS[o] < n)
 
+    def exists_at(slot):
+        there = me + jnp.where(slot < 2, slot - 2, slot - 1)
+        return jnp.logical_and(there >= 0, there < n)
+
     def target(o):
         return {"ctx": me + OFFSETS[o]}
 
     def column(g, width):
         return pl.ds(pl.multiple_of(g * width, width), width)
 
-    def near_copy(g, o, part):
+    core = lax.rem(me, 2)
+    sibling = {"ctx": me + 1 - 2 * core}
+    forward = 3 * (1 - core)
+    passed = 1 + core
+    beside = 2 - core
+
+    def own_part(g, part):
+        return kv.at[:, pl.ds(pl.multiple_of(part * kv_width + g * HEAD, HEAD), HEAD)]
+
+    def remote(src, dst, sent, received, device):
         return pltpu.make_async_remote_copy(
-            src_ref=kv_hbm.at[:, pl.ds(pl.multiple_of(part * kv_width + g * HEAD, HEAD), HEAD)],
-            dst_ref=near.at[g, 3 - o, part],
-            send_sem=near_send.at[g, o, part],
-            recv_sem=near_recv.at[g, 3 - o, part],
-            device_id=target(o),
-            device_id_type=pl.DeviceIdType.MESH,
-        )
-
-    def grad_copy(g, o):
-        return pltpu.make_async_remote_copy(
-            src_ref=gsend.at[g, o],
-            dst_ref=grecv.at[g, 3 - o],
-            send_sem=grad_send.at[g, o],
-            recv_sem=grad_recv.at[g, 3 - o],
-            device_id=target(o),
-            device_id_type=pl.DeviceIdType.MESH,
-        )
+            src_ref=src, dst_ref=dst, send_sem=sent, recv_sem=received,
+            device_id=device, device_id_type=pl.DeviceIdType.MESH,
+        )
+
+    def far_copy(g, o, part):
+        return remote(
+            own_part(g, part), near.at[g, 3 - o, part],
+            near_send.at[g, o, part], near_recv.at[g, 3 - o, part], target(o),
+        )
+
+    def beside_copy(g, part):
+        return remote(
+            own_part(g, part), near.at[g, 1 + core, part],
+            near_send.at[g, 1, part], near_recv.at[g, 1 + core, part], sibling,
+        )
+
+    def relay_copy(g, part):
+        return remote(
+            near.at[g, forward, part], near.at[g, 2 - core, part],
+            near_send.at[g, 2, part], near_recv.at[g, 2 - core, part], sibling,
+        )
+
+    def near_wait(g, slot):
+        for part in range(2):
+            remote(
+                near.at[g, slot, part], near.at[g, slot, part],
+                near_send.at[g, 0, part], near_recv.at[g, slot, part], sibling,
+            ).wait_recv()
+
+    def far_grad(g, o):
+        return remote(
+            gsend.at[g, o], grecv.at[g, 3 - o], grad_send.at[g, o], grad_recv.at[g, 3 - o], target(o)
+        )
+
+    def beside_grad(g):
+        return remote(gsend.at[g, beside], grecv.at[g, 1], grad_send.at[g, 1], grad_recv.at[g, 1], sibling)
+
+    def passed_grad(g):
+        return remote(gsend.at[g, passed], grecv.at[g, 2], grad_send.at[g, 2], grad_recv.at[g, 2], sibling)
+
+    def relay(g):
+        @pl.when(exists_at(forward))
+        def _():
+            near_wait(g, forward)
+            relay_copy(g, 0).start()
+            relay_copy(g, 1).start()
+
+    def combine(g):
+        @pl.when(exists_at(forward))
+        def _():
+            passed_grad(g).wait_recv()
+            both = gsend[g, forward].astype(jnp.float32) + grecv[g, 2].astype(jnp.float32)
+            gsend[g, forward] = both.astype(jnp.bfloat16)
+
+        for o, mine in ((3, 0), (0, 1)):
+
+            @pl.when(jnp.logical_and(exists(o), core == mine))
+            def _():
+                far_grad(g, o).start()
 
     def load_copies(g):
         return (
@@ -70,41 +125,48 @@
 
     kv_load = pltpu.make_async_copy(kv_hbm, kv, kv_sem)
 
+    kv_load.start()
+    for copy in load_copies(0):
+        copy.start()
     barrier = pltpu.get_barrier_semaphore()
-    arrivals = jnp.int32(0)
+    pl.semaphore_signal(barrier, inc=1, device_id=sibling, device_id_type=pl.DeviceIdType.MESH)
+    for o in (0, 3):
+
+        @pl.when(exists(o))
+        def _():
+            pl.semaphore_signal(barrier, inc=1, device_id=target(o), device_id_type=pl.DeviceIdType.MESH)
+
     for o in range(4):
-        there = exists(o)
-        arrivals = arrivals + there.astype(jnp.int32)
-
-        @pl.when(there)
-        def _():
-            pl.semaphore_signal(barrier, inc=1, device_id=target(o), device_id_type=pl.DeviceIdType.MESH)
-
-        @pl.when(jnp.logical_not(there))
+
+        @pl.when(jnp.logical_not(exists(o)))
         def _():
             near[:, o] = jnp.zeros((groups, 2, rows, HEAD), near.dtype)
-            grecv[:, o] = jnp.zeros((groups, 2, rows, HEAD), grecv.dtype)
-
-    kv_load.start()
+            if o in (0, 3):
+                grecv[:, o] = jnp.zeros((groups, 2, rows, HEAD), grecv.dtype)
+
+    kv_load.wait()
+    pl.semaphore_wait(barrier, 1 + exists(0).astype(jnp.int32) + exists(3).astype(jnp.int32))
+
     for g in range(groups):
-        for copy in load_copies(g):
-            copy.start()
-    pl.semaphore_wait(barrier, arrivals)
-
-    for g in range(groups):
-        for o in (3, 0, 2, 1):
+        for o in (3, 0):
 
             @pl.when(exists(o))
             def _():
-                near_copy(g, o, 0).start()
-                near_copy(g, o, 1).start()
+                far_copy(g, o, 0).start()
+                far_copy(g, o, 1).start()
+
+        beside_copy(g, 0).start()
+        beside_copy(g, 1).start()
+        if g > 0:
+            for copy in load_copies(g):
+                copy.start()
 
     own_block = slot_ref[me]
     live_count = count_ref[own_block]
     chosen = []
     bias = []
     for j in (1, 2):
-        wanted = blocks_ref[own_block, j]
+        wanted = blocks_ref[j, own_block]
         hits = []
         for o in range(4):
             there = jnp.clip(me + OFFSETS[o], 0, n - 1)
@@ -112,8 +174,6 @@
         chosen.append(hits)
         bias.append(jnp.where(hits[0] | hits[1] | hits[2] | hits[3], 0.0, NEG).astype(jnp.float32))
 
-    kv_load.wait()
-
     def pick(g, part, hits):
         value = near[g, 0, part]
         for o in range(1, 4):
@@ -123,12 +183,19 @@
     def step(g, carry):
         for copy in load_copies(g):
             copy.wait()
-        for o in range(4):
-
-            @pl.when(exists(3 - o))
-            def _():
-                near_copy(g, o, 0).wait_recv()
-                near_copy(g, o, 1).wait_recv()
+        near_wait(g, beside)
+
+        @pl.when(exists_at(3 - forward))
+        def _():
+            near_wait(g, 3 - forward)
+
+        @pl.when(exists_at(passed))
+        def _():
+            near_wait(g, passed)
+
+        @pl.when(g > 0)
+        def _():
+            combine(g - 1)
 
         own_key = kv[:, pl.ds(pl.multiple_of(g * HEAD, HEAD), HEAD)]
         own_value = kv[:, pl.ds(pl.multiple_of(kv_width + g * HEAD, HEAD), HEAD)]
@@ -161,6 +228,12 @@
             for i in range(2):
                 att[:, pl.ds(starts[i], HEAD)] = mixed[i * rows : (i + 1) * rows]
                 dq[:, pl.ds(starts[i], HEAD)] = query_grad[i * rows : (i + 1) * rows]
+            if pair == 1:
+
+                @pl.when(g + 1 < groups)
+                def _():
+                    relay(g + 1)
+
             key_grad = key_grad + jnp.dot(score_grads, q2, preferred_element_type=jnp.float32)
             value_grad = value_grad + jnp.dot(rounded, do2, preferred_element_type=jnp.float32)
         for part, grad in ((0, key_grad * scale), (1, value_grad)):
@@ -169,28 +242,37 @@
                 gsend[g, o, part] = jnp.where(
                     chosen[0][o], grad[rows : 2 * rows], jnp.where(chosen[1][o], grad[2 * rows :], 0.0)
                 ).astype(jnp.bfloat16)
-        for o in (3, 0, 2, 1):
-
-            @pl.when(exists(o))
-            def _():
-                grad_copy(g, o).start()
-
+        @pl.when(exists_at(passed))
+        def _():
+            passed_grad(g).start()
+
+        for o, mine in ((3, 1), (0, 0)):
+
+            @pl.when(jnp.logical_and(exists(o), core == mine))
+            def _():
+                far_grad(g, o).start()
+
+        beside_grad(g).start()
         for copy in store_copies(g):
             copy.start()
         return carry
 
+    relay(0)
     lax.fori_loop(0, groups, step, 0)
+    combine(groups - 1)
 
     def finish(g, carry):
-        for o in range(4):
+        for o in (0, 3):
 
             @pl.when(exists(3 - o))
             def _():
-                grad_copy(g, o).wait_recv()
+                far_grad(g, o).wait_recv()
+
+        beside_grad(g).wait_recv()
 
         for part in range(2):
             total = own_grad[g, part]
-            for o in range(4):
+            for o in (0, 1, 3):
                 total = total + grecv[g, o, part].astype(jnp.float32)
             kvg[:, pl.ds(pl.multiple_of(part * kv_width + g * HEAD, HEAD), HEAD)] = total.astype(jnp.bfloat16)
         return carry
@@ -200,14 +282,26 @@
     kvg_store.start()
 
     def drain(g, carry):
-        for o in range(4):
+        for o in (0, 3):
 
             @pl.when(exists(o))
             def _():
-                near_copy(g, o, 0).wait_send()
-                near_copy(g, o, 1).wait_send()
-                grad_copy(g, o).wait_send()
-
+                far_copy(g, o, 0).wait_send()
+                far_copy(g, o, 1).wait_send()
+                far_grad(g, o).wait_send()
+
+        @pl.when(exists_at(forward))
+        def _():
+            relay_copy(g, 0).wait_send()
+            relay_copy(g, 1).wait_send()
+
+        @pl.when(exists_at(passed))
+        def _():
+            passed_grad(g).wait_send()
+
+        beside_copy(g, 0).wait_send()
+        beside_copy(g, 1).wait_send()
+        beside_grad(g).wait_send()
         for copy in store_copies(g):
             copy.wait()
         return carry
@@ -235,7 +329,7 @@
             jax.ShapeDtypeStruct((rows, width), jnp.bfloat16),
             jax.ShapeDtypeStruct((rows, 2 * kv_width), jnp.bfloat16),
         ),
-        in_specs=[scalars] * 3 + [anywhere] * 3,
+        in_specs=[scalars] * 3 + [pl.BlockSpec(memory_space=pltpu.HBM)] * 3,
         out_specs=(anywhere, anywhere, anywhere),
         scratch_shapes=[
             wide, narrow, wide, wide, wide, narrow,
@@ -246,7 +340,7 @@
         compiler_params=pltpu.CompilerParams(
             collective_id=0, has_side_effects=True, vmem_limit_bytes=40 * 1024 * 1024
         ),
-    )(key_blocks, key_count, block_at_slot, queries, keys_values, out_grad)
+    )(key_blocks.T, key_count, block_at_slot, queries, keys_values, out_grad)
 
 
 def solution(mesh):

time: 50.3 us -> 40.2 us (0.80)
  the two profiles are of different devices: /device:TPU:20 before, /device:TPU:7 now
where the time goes in v1:
time: 40.2 us; the launch traced here: 39.9 us
  Pallas kernels  31.9 us (79%)
  local copies, waits for them, and re-layouts  7.38 us (18%)
  between operations  0.66 us (2%)
    pallas_call x1, Pallas kernels, body(): pl.pallas_call(functools.partial(kernel, n, groups, repeats), out_shape=(...  31.9 us
    unnamed x15, local copies, waits for them, and re-layouts  7.38 us

profile of v1, /device:TPU:7, one launch (start us, length us, event | category | flops | bytes accessed | tf_op | source)
XLA Modules:
  0.0 39.9 jit_solution(17285420207796868498)
XLA Ops:
  0.6 0.0 copy-start.5
  0.6 0.0 copy-start.4
  0.7 0.6 %copy-done.5 = s32[16]{0:T(128)S(1)} copy-done((s32[16]{0:T(128)S(1)}, s32[16]{0:T(128)}, u32[]{:S(2)}) %copy-start.5) | copy-done | bytes 88
  1.3 0.0 copy-done.4
  1.3 0.0 copy-start
  1.3 1.2 %copy-done = bf16[128,4096]{1,0:T(8,128)(2,1)S(1)} copy-done((bf16[128,4096]{1,0:T(8,128)(2,1)S(1)}, bf16[128,4096]{1,0:T(8,128)(2,1)}, u32[]{:S(2)}) %copy-start) | copy-done | bytes 1048600
  2.5 0.0 copy-start.1
  2.5 1.2 %copy-done.1 = bf16[128,4096]{1,0:T(8,128)(2,1)S(1)} copy-done((bf16[128,4096]{1,0:T(8,128)(2,1)S(1)}, bf16[128,4096]{1,0:T(8,128)(2,1)}, u32[]{:S(2)}) %copy-start.1) | copy-done | bytes 1048600
  3.8 0.0 copy-start.2
  3.8 0.9 %copy-done.2 = bf16[128,1024]{1,0:T(8,128)(2,1)S(1)} copy-done((bf16[128,1024]{1,0:T(8,128)(2,1)S(1)}, bf16[128,1024]{1,0:T(8,128)(2,1)}, u32[]{:S(2)}) %copy-start.2) | copy-done | bytes 262168
  4.7 0.0 copy-start.3
  4.7 0.7 %copy-done.3 = s32[16,3]{0,1:T(4,128)S(1)} copy-done((s32[16,3]{0,1:T(4,128)S(1)}, s32[16,3]{0,1:T(4,128)}, u32[]{:S(2)}) %copy-start.3) | copy-done | bytes 216
  5.4 31.9 %shard_map.85 = (bf16[128,4096]{1,0:T(8,128)(2,1)S(1)}, bf16[128,4096]{1,0:T(8,128)(2,1)S(1)}, bf16[128,1024]{1,0:T(8,128)(2,1)S(1)}) custom-call(s32[3,16]{1,0:T(4,128)S(1)} %bitcast.1, s32[16]{0:T(128)S(1)} %copy-done.4, s32[16]{0:T(128)S(1)} %copy-done.5, bf16[128,4096]{1,0:T(8,128)(2,1)S(1)} %copy-done, bf16[128,1024]{1,0:T(8,128)(2,1)S(1)} %copy-done.2, ...), custom_call_target="tpu_custom_call" | custom-call | tf_op jit(solution)/shard_map/pallas_call | solution.py:325
  37.2 1.0 %copy.12 = bf16[128,4096]{1,0:T(8,128)(2,1)} copy(bf16[128,4096]{1,0:T(8,128)(2,1)S(1)} %get-tuple-element.6) | data formatting | bytes 2097152
  38.2 1.0 %copy.13 = bf16[128,4096]{1,0:T(8,128)(2,1)} copy(bf16[128,4096]{1,0:T(8,128)(2,1)S(1)} %get-tuple-element.7) | data formatting | bytes 2097152
  39.2 0.7 %copy.14 = bf16[128,1024]{1,0:T(8,128)(2,1)} copy(bf16[128,1024]{1,0:T(8,128)(2,1)S(1)} %get-tuple-element.8) | data formatting | bytes 524288
Async XLA Ops:
  0.6 0.7 %copy-start.5 = (s32[16]{0:T(128)S(1)}, s32[16]{0:T(128)}, u32[]{:S(2)}) copy-start(s32[16]{0:T(128)} %slot_ref.1) | copy-start | bytes 196
  0.6 0.7 %copy-start.4 = (s32[16]{0:T(128)S(1)}, s32[16]{0:T(128)}, u32[]{:S(2)}) copy-start(s32[16]{0:T(128)} %count_ref.1) | copy-start | bytes 196
  1.3 1.2 %copy-start = (bf16[128,4096]{1,0:T(8,128)(2,1)S(1)}, bf16[128,4096]{1,0:T(8,128)(2,1)}, u32[]{:S(2)}) copy-start(bf16[128,4096]{1,0:T(8,128)(2,1)} %q_hbm.1) | copy-start | bytes 3145732
  2.5 1.2 %copy-start.1 = (bf16[128,4096]{1,0:T(8,128)(2,1)S(1)}, bf16[128,4096]{1,0:T(8,128)(2,1)}, u32[]{:S(2)}) copy-start(bf16[128,4096]{1,0:T(8,128)(2,1)} %do_hbm.1) | copy-start | bytes 3145732
  3.8 0.9 %copy-start.2 = (bf16[128,1024]{1,0:T(8,128)(2,1)S(1)}, bf16[128,1024]{1,0:T(8,128)(2,1)}, u32[]{:S(2)}) copy-start(bf16[128,1024]{1,0:T(8,128)(2,1)} %kv_hbm.1) | copy-start | bytes 786436
  4.7 0.7 %copy-start.3 = (s32[16,3]{0,1:T(4,128)S(1)}, s32[16,3]{0,1:T(4,128)}, u32[]{:S(2)}) copy-start(s32[16,3]{0,1:T(4,128)} %param.9) | copy-start | bytes 580

commit v2 on v1

--- a/solution.py
+++ b/solution.py
@@ -46,39 +46,34 @@
     passed = 1 + core
     beside = 2 - core
 
-    def own_part(g, part):
-        return kv.at[:, pl.ds(pl.multiple_of(part * kv_width + g * HEAD, HEAD), HEAD)]
-
     def remote(src, dst, sent, received, device):
         return pltpu.make_async_remote_copy(
             src_ref=src, dst_ref=dst, send_sem=sent, recv_sem=received,
             device_id=device, device_id_type=pl.DeviceIdType.MESH,
         )
 
-    def far_copy(g, o, part):
+    def far_copy(g, o):
+        return remote(kv.at[g], near.at[g, 3 - o], near_send.at[g, o], near_recv.at[g, 3 - o], target(o))
+
+    def beside_copy(g):
         return remote(
-            own_part(g, part), near.at[g, 3 - o, part],
-            near_send.at[g, o, part], near_recv.at[g, 3 - o, part], target(o),
-        )
-
-    def beside_copy(g, part):
+            kv.at[g], near.at[g, 1 + core], near_send.at[g, 1], near_recv.at[g, 1 + core], sibling
+        )
+
+    def relay_copy(g):
         return remote(
-            own_part(g, part), near.at[g, 1 + core, part],
-            near_send.at[g, 1, part], near_recv.at[g, 1 + core, part], sibling,
-        )
-
-    def relay_copy(g, part):
-        return remote(
-            near.at[g, forward, part], near.at[g, 2 - core, part],
-            near_send.at[g, 2, part], near_recv.at[g, 2 - core, part], sibling,
+            near.at[g, forward], near.at[g, 2 - core], near_send.at[g, 2], near_recv.at[g, 2 - core], sibling
         )
 
     def near_wait(g, slot):
-        for part in range(2):
-            remote(
-                near.at[g, slot, part], near.at[g, slot, part],
-                near_send.at[g, 0, part], near_recv.at[g, slot, part], sibling,
-            ).wait_recv()
+        remote(
+            near.at[g, slot], near.at[g, slot], near_send.at[g, 0], near_recv.at[g, slot], sibling
+        ).wait_recv()
+
+    def kv_load(g, part):
+        return pltpu.make_async_copy(
+            kv_hbm.at[:, pl.ds(part * kv_width + g * HEAD, HEAD)], kv.at[g, part], kv_sem.at[g, part]
+        )
 
     def far_grad(g, o):
         return remote(
@@ -95,8 +90,7 @@
         @pl.when(exists_at(forward))
         def _():
             near_wait(g, forward)
-            relay_copy(g, 0).start()
-            relay_copy(g, 1).start()
+            relay_copy(g).start()
 
     def combine(g):
         @pl.when(exists_at(forward))
@@ -123,9 +117,9 @@
             pltpu.make_async_copy(dq.at[:, column(g, wide)], dq_hbm.at[:, column(g, wide)], out_sem.at[g, 1]),
         )
 
-    kv_load = pltpu.make_async_copy(kv_hbm, kv, kv_sem)
-
-    kv_load.start()
+    for g in range(groups):
+        for part in range(2):
+            kv_load(g, part).start()
     for copy in load_copies(0):
         copy.start()
     barrier = pltpu.get_barrier_semaphore()
@@ -144,19 +138,18 @@
             if o in (0, 3):
                 grecv[:, o] = jnp.zeros((groups, 2, rows, HEAD), grecv.dtype)
 
-    kv_load.wait()
     pl.semaphore_wait(barrier, 1 + exists(0).astype(jnp.int32) + exists(3).astype(jnp.int32))
 
     for g in range(groups):
+        kv_load(g, 0).wait()
+        kv_load(g, 1).wait()
         for o in (3, 0):
 
             @pl.when(exists(o))
             def _():
-                far_copy(g, o, 0).start()
-                far_copy(g, o, 1).start()
-
-        beside_copy(g, 0).start()
-        beside_copy(g, 1).start()
+                far_copy(g, o).start()
+
+        beside_copy(g).start()
         if g > 0:
             for copy in load_copies(g):
                 copy.start()
@@ -197,8 +190,8 @@
         def _():
             combine(g - 1)
 
-        own_key = kv[:, pl.ds(pl.multiple_of(g * HEAD, HEAD), HEAD)]
-        own_value = kv[:, pl.ds(pl.multiple_of(kv_width + g * HEAD, HEAD), HEAD)]
+        own_key = kv[g, 0]
+        own_value = kv[g, 1]
         keys = jnp.concatenate([own_key, pick(g, 0, chosen[0]), pick(g, 0, chosen[1])], axis=0)
         values = jnp.concatenate([own_value, pick(g, 1, chosen[0]), pick(g, 1, chosen[1])], axis=0)
         keys_t = keys.T
@@ -286,21 +279,18 @@
 
             @pl.when(exists(o))
             def _():
-                far_copy(g, o, 0).wait_send()
-                far_copy(g, o, 1).wait_send()
+                far_copy(g, o).wait_send()
                 far_grad(g, o).wait_send()
 
         @pl.when(exists_at(forward))
         def _():
-            relay_copy(g, 0).wait_send()
-            relay_copy(g, 1).wait_send()
+            relay_copy(g).wait_send()
 
         @pl.when(exists_at(passed))
         def _():
             passed_grad(g).wait_send()
 
-        beside_copy(g, 0).wait_send()
-        beside_copy(g, 1).wait_send()
+        beside_copy(g).wait_send()
         beside_grad(g).wait_send()
         for copy in store_copies(g):
             copy.wait()
@@ -308,6 +298,17 @@
 
     lax.fori_loop(0, groups, drain, 0)
     kvg_store.wait()
+
+
+def flush(att, dq, kvg, att_out, dq_out, kvg_out, sem):
+    copies = [
+        pltpu.make_async_copy(source, result, sem.at[i])
+        for i, (source, result) in enumerate(((att, att_out), (dq, dq_out), (kvg, kvg_out)))
+    ]
+    for copy in copies:
+        copy.start()
+    for copy in copies:
+        copy.wait()
 
 
 def body(queries, keys_values, out_grad, key_blocks, key_count, block_at_slot):
@@ -322,25 +323,34 @@
     narrow = pltpu.VMEM((rows, 2 * kv_width), jnp.bfloat16)
     ring = pltpu.VMEM((groups, 4, 2, rows, HEAD), jnp.bfloat16)
     dma = pltpu.SemaphoreType.DMA
-    return pl.pallas_call(
+    shapes = (
+        jax.ShapeDtypeStruct((rows, width), jnp.bfloat16),
+        jax.ShapeDtypeStruct((rows, width), jnp.bfloat16),
+        jax.ShapeDtypeStruct((rows, 2 * kv_width), jnp.bfloat16),
+    )
+    results = pl.pallas_call(
         functools.partial(kernel, n, groups, repeats),
-        out_shape=(
-            jax.ShapeDtypeStruct((rows, width), jnp.bfloat16),
-            jax.ShapeDtypeStruct((rows, width), jnp.bfloat16),
-            jax.ShapeDtypeStruct((rows, 2 * kv_width), jnp.bfloat16),
-        ),
+        out_shape=shapes,
         in_specs=[scalars] * 3 + [pl.BlockSpec(memory_space=pltpu.HBM)] * 3,
         out_specs=(anywhere, anywhere, anywhere),
         scratch_shapes=[
-            wide, narrow, wide, wide, wide, narrow,
+            wide, pltpu.VMEM((groups, 2, rows, HEAD), jnp.bfloat16), wide, wide, wide, narrow,
             ring, pltpu.VMEM((groups, 2, rows, HEAD), jnp.float32), ring, ring,
-            dma((groups, 2)), dma, dma((groups, 2)), dma,
-            dma((groups, 4, 2)), dma((groups, 4, 2)), dma((groups, 4)), dma((groups, 4)),
+            dma((groups, 2)), dma((groups, 2)), dma((groups, 2)), dma,
+            dma((groups, 4)), dma((groups, 4)), dma((groups, 4)), dma((groups, 4)),
         ],
         compiler_params=pltpu.CompilerParams(
             collective_id=0, has_side_effects=True, vmem_limit_bytes=40 * 1024 * 1024
         ),
     )(key_blocks.T, key_count, block_at_slot, queries, keys_values, out_grad)
+    return pl.pallas_call(
+        flush,
+        out_shape=shapes,
+        in_specs=[anywhere] * 3,
+        out_specs=(pl.BlockSpec(memory_space=pltpu.HBM),) * 3,
+        scratch_shapes=[dma((3,))],
+        compiler_params=pltpu.CompilerParams(vmem_limit_bytes=1024 * 1024),
+    )(*results)
 
 
 def solution(mesh):

time: 40.2 us -> 38.7 us (0.963)
  local copies, waits for them, and re-layouts: 7.38 us -> 4.73 us
  Pallas kernels: 31.9 us -> 33.1 us
    unnamed x15 -> x12, local copies, waits for them, and re-layouts: 7.38 us -> 4.73 us
    pallas_call x1 -> x2, Pallas kernels: 31.9 us -> 33.1 us  [the longest x1 31.6 us: body(): pl.pallas_call(functools.partial(kernel, n, groups, repeats), out_shape=s...]
where the time goes in v2:
time: 38.7 us; the launch traced here: 38.5 us
  Pallas kernels  33.1 us (86%)
  local copies, waits for them, and re-layouts  4.73 us (12%)
  between operations  0.66 us (2%)
    pallas_call x1, Pallas kernels, body(): pl.pallas_call(functools.partial(kernel, n, groups, repeats), out_shape=s...  31.6 us
    unnamed x12, local copies, waits for them, and re-layouts  4.73 us
    pallas_call x1, Pallas kernels, body(): pl.pallas_call(flush, out_shape=shapes, in_specs=[anywhere] * 3, out_spec...  1.42 us

profile of v2, /device:TPU:7, one launch (start us, length us, event | category | flops | bytes accessed | tf_op | source)
XLA Modules:
  0.0 38.5 jit_solution(4262864291530686689)
XLA Ops:
  0.6 0.0 copy-start.5
  0.6 0.0 copy-start.4
  0.7 0.6 %copy-done.5 = s32[16]{0:T(128)S(1)} copy-done((s32[16]{0:T(128)S(1)}, s32[16]{0:T(128)}, u32[]{:S(2)}) %copy-start.5) | copy-done | bytes 88
  1.3 0.0 copy-done.4
  1.3 0.0 copy-start
  1.3 1.2 %copy-done = bf16[128,4096]{1,0:T(8,128)(2,1)S(1)} copy-done((bf16[128,4096]{1,0:T(8,128)(2,1)S(1)}, bf16[128,4096]{1,0:T(8,128)(2,1)}, u32[]{:S(2)}) %copy-start) | copy-done | bytes 1048600
  2.5 0.0 copy-start.1
  2.5 1.2 %copy-done.1 = bf16[128,4096]{1,0:T(8,128)(2,1)S(1)} copy-done((bf16[128,4096]{1,0:T(8,128)(2,1)S(1)}, bf16[128,4096]{1,0:T(8,128)(2,1)}, u32[]{:S(2)}) %copy-start.1) | copy-done | bytes 1048600
  3.8 0.0 copy-start.2
  3.8 0.9 %copy-done.2 = bf16[128,1024]{1,0:T(8,128)(2,1)S(1)} copy-done((bf16[128,1024]{1,0:T(8,128)(2,1)S(1)}, bf16[128,1024]{1,0:T(8,128)(2,1)}, u32[]{:S(2)}) %copy-start.2) | copy-done | bytes 262168
  4.7 0.0 copy-start.3
  4.7 0.7 %copy-done.3 = s32[16,3]{0,1:T(4,128)S(1)} copy-done((s32[16,3]{0,1:T(4,128)S(1)}, s32[16,3]{0,1:T(4,128)}, u32[]{:S(2)}) %copy-start.3) | copy-done | bytes 216
  5.4 31.6 %shard_map.85 = (bf16[128,4096]{1,0:T(8,128)(2,1)S(1)}, bf16[128,4096]{1,0:T(8,128)(2,1)S(1)}, bf16[128,1024]{1,0:T(8,128)(2,1)S(1)}) custom-call(s32[3,16]{1,0:T(4,128)S(1)} %bitcast.1, s32[16]{0:T(128)S(1)} %copy-done.4, s32[16]{0:T(128)S(1)} %copy-done.5, bf16[128,4096]{1,0:T(8,128)(2,1)S(1)} %copy-done, bf16[128,1024]{1,0:T(8,128)(2,1)S(1)} %copy-done.2, ...), custom_call_target="tpu_custom_call" | custom-call | tf_op jit(solution)/shard_map/pallas_call | solution.py:331
  37.0 1.4 %shard_map.86 = (bf16[128,4096]{1,0:T(8,128)(2,1)}, bf16[128,4096]{1,0:T(8,128)(2,1)}, bf16[128,1024]{1,0:T(8,128)(2,1)}) custom-call(bf16[128,4096]{1,0:T(8,128)(2,1)S(1)} %get-tuple-element.6.att, bf16[128,4096]{1,0:T(8,128)(2,1)S(1)} %get-tuple-element.7.dq, bf16[128,1024]{1,0:T(8,128)(2,1)S(1)} %get-tuple-element.8.kvg), custom_call_target="tpu_custom_call" | custom-call | tf_op jit(solution)/shard_map/pallas_call | solution.py:346
Async XLA Ops:
  0.6 0.7 %copy-start.5 = (s32[16]{0:T(128)S(1)}, s32[16]{0:T(128)}, u32[]{:S(2)}) copy-start(s32[16]{0:T(128)} %slot_ref.1) | copy-start | bytes 196
  0.6 0.7 %copy-start.4 = (s32[16]{0:T(128)S(1)}, s32[16]{0:T(128)}, u32[]{:S(2)}) copy-start(s32[16]{0:T(128)} %count_ref.1) | copy-start | bytes 196
  1.3 1.2 %copy-start = (bf16[128,4096]{1,0:T(8,128)(2,1)S(1)}, bf16[128,4096]{1,0:T(8,128)(2,1)}, u32[]{:S(2)}) copy-start(bf16[128,4096]{1,0:T(8,128)(2,1)} %q_hbm.1) | copy-start | bytes 3145732
  2.5 1.2 %copy-start.1 = (bf16[128,4096]{1,0:T(8,128)(2,1)S(1)}, bf16[128,4096]{1,0:T(8,128)(2,1)}, u32[]{:S(2)}) copy-start(bf16[128,4096]{1,0:T(8,128)(2,1)} %do_hbm.1) | copy-start | bytes 3145732
  3.8 0.9 %copy-start.2 = (bf16[128,1024]{1,0:T(8,128)(2,1)S(1)}, bf16[128,1024]{1,0:T(8,128)(2,1)}, u32[]{:S(2)}) copy-start(bf16[128,1024]{1,0:T(8,128)(2,1)} %kv_hbm.1) | copy-start | bytes 786436
  4.7 0.7 %copy-start.3 = (s32[16,3]{0,1:T(4,128)S(1)}, s32[16,3]{0,1:T(4,128)}, u32[]{:S(2)}) copy-start(s32[16,3]{0,1:T(4,128)} %param.9) | copy-start | bytes 580

commit v3 on v2

--- a/solution.py
+++ b/solution.py
@@ -300,15 +300,26 @@
     kvg_store.wait()
 
 
-def flush(att, dq, kvg, att_out, dq_out, kvg_out, sem):
-    copies = [
-        pltpu.make_async_copy(source, result, sem.at[i])
-        for i, (source, result) in enumerate(((att, att_out), (dq, dq_out), (kvg, kvg_out)))
-    ]
-    for copy in copies:
-        copy.start()
-    for copy in copies:
-        copy.wait()
+def flush(att, dq, kvg, att_out, dq_out, kvg_out, att_held, dq_held, kvg_held, in_sem, out_sem):
+    width = kvg.shape[1]
+    pieces = []
+    for start in range(0, att.shape[1], width):
+        pieces.append((att, att_held, att_out, start))
+        pieces.append((dq, dq_held, dq_out, start))
+    pieces.append((kvg, kvg_held, kvg_out, 0))
+    loads = []
+    stores = []
+    for i, (source, held, result, start) in enumerate(pieces):
+        part = pl.ds(start, width)
+        loads.append(pltpu.make_async_copy(source.at[:, part], held.at[:, part], in_sem.at[i]))
+        stores.append(pltpu.make_async_copy(held.at[:, part], result.at[:, part], out_sem.at[i]))
+    for load in loads:
+        load.start()
+    for load, store in zip(loads, stores):
+        load.wait()
+        store.start()
+    for store in stores:
+        store.wait()
 
 
 def body(queries, keys_values, out_grad, key_blocks, key_count, block_at_slot):
@@ -328,6 +339,7 @@
         jax.ShapeDtypeStruct((rows, width), jnp.bfloat16),
         jax.ShapeDtypeStruct((rows, 2 * kv_width), jnp.bfloat16),
     )
+    pieces = 2 * (width // (2 * kv_width)) + 1
     results = pl.pallas_call(
         functools.partial(kernel, n, groups, repeats),
         out_shape=shapes,
@@ -340,7 +352,7 @@
             dma((groups, 4)), dma((groups, 4)), dma((groups, 4)), dma((groups, 4)),
         ],
         compiler_params=pltpu.CompilerParams(
-            collective_id=0, has_side_effects=True, vmem_limit_bytes=40 * 1024 * 1024
+            collective_id=0, has_side_effects=True, vmem_limit_bytes=60 * 1024 * 1024
         ),
     )(key_blocks.T, key_count, block_at_slot, queries, keys_values, out_grad)
     return pl.pallas_call(
@@ -348,8 +360,8 @@
         out_shape=shapes,
         in_specs=[anywhere] * 3,
         out_specs=(pl.BlockSpec(memory_space=pltpu.HBM),) * 3,
-        scratch_shapes=[dma((3,))],
-        compiler_params=pltpu.CompilerParams(vmem_limit_bytes=1024 * 1024),
+        scratch_shapes=[wide, wide, narrow, dma((pieces,)), dma((pieces,))],
+        compiler_params=pltpu.CompilerParams(vmem_limit_bytes=60 * 1024 * 1024),
     )(*results)
 
 

time: 38.7 us -> 35.6 us (0.920)
  local copies, waits for them, and re-layouts: 4.73 us -> 0 us
  Pallas kernels: 33.1 us -> 34.8 us
    unnamed x12 -> x0, local copies, waits for them, and re-layouts: 4.73 us -> none
    pallas_call x1, Pallas kernels: 1.42 us -> 2.5 us  [body(): pl.pallas_call(flush, out_shape=shapes, in_specs=[anywhere] * 3, out_spec...]
    pallas_call x1, Pallas kernels: 31.6 us -> 32.3 us  [body(): pl.pallas_call(functools.partial(kernel, n, groups, repeats), out_shape=s...]
where the time goes in v3:
time: 35.6 us; the launch traced here: 35.5 us
  Pallas kernels  34.8 us (98%)
  between operations  0.64 us (2%)
    pallas_call x1, Pallas kernels, body(): pl.pallas_call(functools.partial(kernel, n, groups, repeats), out_shape=s...  32.3 us
    pallas_call x1, Pallas kernels, body(): pl.pallas_call(flush, out_shape=shapes, in_specs=[anywhere] * 3, out_spec...  2.5 us

profile of v3, /device:TPU:7, one launch (start us, length us, event | category | flops | bytes accessed | tf_op | source)
XLA Modules:
  0.0 35.5 jit_solution(15299699563017033933)
XLA Ops:
  0.6 32.3 %shard_map.85 = (bf16[128,4096]{1,0:T(8,128)(2,1)}, bf16[128,4096]{1,0:T(8,128)(2,1)}, bf16[128,1024]{1,0:T(8,128)(2,1)}) custom-call(s32[3,16]{1,0:T(4,128)} %bitcast.1, s32[16]{0:T(128)} %count_ref.1, s32[16]{0:T(128)} %slot_ref.1, bf16[128,4096]{1,0:T(8,128)(2,1)} %q_hbm.1, bf16[128,1024]{1,0:T(8,128)(2,1)} %kv_hbm.1, bf16[128,4096]{1,0:T(8,128)(2,1)} %do_hbm.1), custom_call_target="tpu_custom_call" | custom-call | tf_op jit(solution)/shard_map/pallas_call | solution.py:343
  33.0 2.5 %shard_map.86 = (bf16[128,4096]{1,0:T(8,128)(2,1)}, bf16[128,4096]{1,0:T(8,128)(2,1)}, bf16[128,1024]{1,0:T(8,128)(2,1)}) custom-call(bf16[128,4096]{1,0:T(8,128)(2,1)} %get-tuple-element.6.att, bf16[128,4096]{1,0:T(8,128)(2,1)} %get-tuple-element.7.dq, bf16[128,1024]{1,0:T(8,128)(2,1)} %get-tuple-element.8.kvg), custom_call_target="tpu_custom_call" | custom-call | tf_op jit(solution)/shard_map/pallas_call | solution.py:358

commit v4 on v3

--- a/solution.py
+++ b/solution.py
@@ -301,12 +301,13 @@
 
 
 def flush(att, dq, kvg, att_out, dq_out, kvg_out, att_held, dq_held, kvg_held, in_sem, out_sem):
-    width = kvg.shape[1]
+    width = kvg.shape[1] // 2
     pieces = []
     for start in range(0, att.shape[1], width):
         pieces.append((att, att_held, att_out, start))
         pieces.append((dq, dq_held, dq_out, start))
-    pieces.append((kvg, kvg_held, kvg_out, 0))
+    for start in range(0, kvg.shape[1], width):
+        pieces.append((kvg, kvg_held, kvg_out, start))
     loads = []
     stores = []
     for i, (source, held, result, start) in enumerate(pieces):
@@ -339,7 +340,7 @@
         jax.ShapeDtypeStruct((rows, width), jnp.bfloat16),
         jax.ShapeDtypeStruct((rows, 2 * kv_width), jnp.bfloat16),
     )
-    pieces = 2 * (width // (2 * kv_width)) + 1
+    pieces = 2 * (width // kv_width) + 2
     results = pl.pallas_call(
         functools.partial(kernel, n, groups, repeats),
         out_shape=shapes,

time: 35.6 us -> 35.8 us (level)
  no operation moved by 1% of the time
where the time goes in v4:
time: 35.8 us; the launch traced here: 35.7 us
  Pallas kernels  35 us (98%)
  between operations  0.64 us (2%)
    pallas_call x1, Pallas kernels, body(): pl.pallas_call(functools.partial(kernel, n, groups, repeats), out_shape=s...  32.3 us
    pallas_call x1, Pallas kernels, body(): pl.pallas_call(flush, out_shape=shapes, in_specs=[anywhere] * 3, out_spec...  2.7 us

profile of v4, /device:TPU:7, one launch (start us, length us, event | category | flops | bytes accessed | tf_op | source)
XLA Modules:
  0.0 35.7 jit_solution(5906188134669765269)
XLA Ops:
  0.6 32.3 %shard_map.85 = (bf16[128,4096]{1,0:T(8,128)(2,1)}, bf16[128,4096]{1,0:T(8,128)(2,1)}, bf16[128,1024]{1,0:T(8,128)(2,1)}) custom-call(s32[3,16]{1,0:T(4,128)} %bitcast.1, s32[16]{0:T(128)} %count_ref.1, s32[16]{0:T(128)} %slot_ref.1, bf16[128,4096]{1,0:T(8,128)(2,1)} %q_hbm.1, bf16[128,1024]{1,0:T(8,128)(2,1)} %kv_hbm.1, bf16[128,4096]{1,0:T(8,128)(2,1)} %do_hbm.1), custom_call_target="tpu_custom_call" | custom-call | tf_op jit(solution)/shard_map/pallas_call | solution.py:344
  33.0 2.7 %shard_map.86 = (bf16[128,4096]{1,0:T(8,128)(2,1)}, bf16[128,4096]{1,0:T(8,128)(2,1)}, bf16[128,1024]{1,0:T(8,128)(2,1)}) custom-call(bf16[128,4096]{1,0:T(8,128)(2,1)} %get-tuple-element.6.att, bf16[128,4096]{1,0:T(8,128)(2,1)} %get-tuple-element.7.dq, bf16[128,1024]{1,0:T(8,128)(2,1)} %get-tuple-element.8.kvg), custom_call_target="tpu_custom_call" | custom-call | tf_op jit(solution)/shard_map/pallas_call | solution.py:359
